TPU v7x, 32 devices: a whole 2x2x4 slice. The times are simulated.
32 devices in a mesh: grp: 2 (over y), frm: 4 (over z), row: 4 (over x, core).
Axes of the slice: x: 2, y: 2, z: 4, core: 2. Of those that a mesh axis runs over, the one named last changes fastest.
Arguments:
- queries: bfloat16 [16, 8, 128, 2240], P(('grp', 'frm'), 'row'), parts along dimension 0, may hold values from -6 to 6
- keys: bfloat16 [16, 8, 128, 2240], P(('grp', 'frm'), 'row'), parts along dimension 0, may hold values from -6 to 6
- values: bfloat16 [16, 8, 128, 2240], P(('grp', 'frm'), 'row'), parts along dimension 0, may hold values from -6 to 6
- flags: int32 [16], P(('grp', 'frm')), parts along dimension 0, may hold values 0 or 1
- blocks: int32 [16], P(('grp', 'frm')), parts along dimension 0, may hold values from 0 to 2, as said below
- out_weight: bfloat16 [2240, 2240], P('frm'), may hold values from -0.125 to 0.125
- norm_gain: float32 [2240], replicated, may hold values from 0.1 to 1.9
Outputs:
- projected: bfloat16 [16, 8, 128, 2240], P(('grp', 'frm'), 'row'), parts along dimension 0
There are 2 independent parts, one for each index of `grp`. A program takes and returns all parts, laid end to end along the dimension named above; an argument that names none is the same for every part. Nothing has to cross between parts.
Inputs may be any that keep to these rules, and one draw needn't show every extreme that they name: `flags`: 1 marks a clean frame, 0 a noisy one. `blocks`: within the 8 frames of one group, block numbers never fall and each block is 1 to 4 consecutive frames, some block exactly 4; every number from 0 to 2 occurs.
All inputs are finite; a program needn't handle non-finite values. No bound on the sum of `flags` on one device may be relied on, other than what follows from the above.
Results may differ from a plain program's by a relative error of at most 0.0049.
Values may be sent and summed in bfloat16 or wider, within the bound.
No kernel may reach another device: no remote copies, remote signals or barrier semaphores. Data moves between devices by JAX's collectives and lax.ppermute only.
A program may use at most 192 MiB of HBM per device.

v0:
```python
import jax
import jax.numpy as jnp
from jax import lax
from jax.sharding import PartitionSpec as P

HEADS = 20
HD = 112
norm_eps = 1e-06


def entering(part, axis, combine, identity):
    place = lax.axis_index(axis)
    gathered = jax.tree.map(lambda a: lax.all_gather(a, axis), part)
    state = jax.tree.map(lambda a, e: jnp.zeros_like(a) + jnp.asarray(e, a.dtype), part, identity)

    def one(step, state):
        return combine(
            state, jax.tree.map(lambda a: lax.dynamic_index_in_dim(a, step, 0, False), gathered)
        )

    return lax.fori_loop(0, place, one, state)


def combine(earlier, later):
    closed_a, opened_a, latest_a = earlier
    closed_b, opened_b, latest_b = later
    advance = (latest_a < latest_b).astype(jnp.float32)
    return (
        closed_a + closed_b + advance * opened_a,
        opened_b + (1.0 - advance) * opened_a,
        jnp.maximum(latest_a, latest_b),
    )


def empty_carry(length):
    return (
        jnp.zeros((length,), jnp.float32),
        jnp.zeros((length,), jnp.float32),
        jnp.full((1,), -1.0, jnp.float32),
    )


def frame_element(frame_states, flag_values, block_values, frame_idx):
    length = frame_states.shape[1]
    return (
        jnp.zeros((length,), jnp.float32),
        flag_values[frame_idx] * frame_states[frame_idx],
        block_values[frame_idx : frame_idx + 1],
    )


def fold_frames(frame_states, flag_values, block_values):
    running = empty_carry(frame_states.shape[1])
    for frame_idx in range(frame_states.shape[0]):
        running = combine(
            running, frame_element(frame_states, flag_values, block_values, frame_idx)
        )
    return running


def read_frames(prefix, frame_states, flag_values, block_values):
    running = prefix
    collected = []
    for frame_idx in range(frame_states.shape[0]):
        advance = (running[2] < block_values[frame_idx : frame_idx + 1]).astype(jnp.float32)
        select = jnp.maximum(advance, flag_values[frame_idx])
        collected.append(running[0] + select * running[1] + frame_states[frame_idx])
        running = combine(
            running, frame_element(frame_states, flag_values, block_values, frame_idx)
        )
    return jnp.stack(collected)


def local(queries, keys, values, flags, blocks, out_weight, norm_gain):
    frames, lat_rows, lat_cols, model_width = queries.shape
    tokens = lat_rows * lat_cols
    key_pos = jax.nn.relu(keys).reshape(frames, tokens, HEADS, HD)
    value_heads = values.reshape(frames, tokens, HEADS, HD)
    partial_value = jnp.einsum(
        "ftha,fthb->fhab", key_pos, value_heads, preferred_element_type=jnp.float32
    )
    partial_value = partial_value.reshape(frames, HEADS * HD * HD)
    flag_values = flags.astype(jnp.float32)
    block_values = blocks.astype(jnp.float32)
    summed = lax.psum(partial_value, "row")
    totals = fold_frames(summed, flag_values, block_values)
    prefix = entering(
        (totals[0], totals[1], totals[2]), "frm", combine, empty_carry(summed.shape[1])
    )
    read_states = read_frames(prefix, summed, flag_values, block_values)
    read_tensor = read_states.reshape(frames, HEADS, HD, HD)
    query_pos = jax.nn.relu(queries).reshape(frames, tokens, HEADS, HD).astype(jnp.float32)
    attended = jnp.einsum(
        "ftha,fhab->fthb", query_pos, read_tensor, precision=lax.Precision.HIGHEST
    )
    inv_rms = lax.rsqrt(jnp.mean(attended * attended, axis=-1, keepdims=True) + norm_eps)
    gain_table = norm_gain.reshape(HEADS, HD)
    normed = (
        (attended * inv_rms * gain_table).astype(jnp.bfloat16).reshape(frames * tokens, model_width)
    )
    projected = jnp.dot(
        normed,
        lax.all_gather(out_weight, "frm", axis=0, tiled=True),
        preferred_element_type=jnp.float32,
    )
    return projected.astype(jnp.bfloat16).reshape(frames, lat_rows, lat_cols, model_width)


def solution(mesh):
    in_specs = (
        P(("grp", "frm"), "row", None, None),
        P(("grp", "frm"), "row", None, None),
        P(("grp", "frm"), "row", None, None),
        P(("grp", "frm")),
        P(("grp", "frm")),
        P("frm", None),
        P(),
    )
    out_specs = P(("grp", "frm"), "row", None, None)
    return jax.shard_map(local, mesh=mesh, in_specs=in_specs, out_specs=out_specs, check_vma=False)
```

profile of v0, /device:TPU:0, one launch (start us, length us, event | category | flops | bytes accessed | tf_op | source)
XLA Modules:
  0.0 476.6 jit_solution(3732474962754750551)
XLA Ops:
  6.5 1.8 broadcast_maximum_fusion.1
  8.3 10.3 %copy.16 = bf16[2,2,128,2240]{2,1,3,0:T(2,128)(2,1)} copy(bf16[2,2,128,2240]{2,3,1,0:T(8,128)(2,1)S(1)} %broadcast_maximum_fusion.1) | data formatting | bytes 4587520 | tf_op jit(solution)/shard_map/jit(relu)/max | solution.py:77
  18.7 5.2 %reshape.37 = bf16[2,256,20,112]{1,3,2,0:T(8,128)(2,1)S(1)} reshape(bf16[2,2,128,2240]{2,1,3,0:T(2,128)(2,1)} %copy.16) | data formatting | bytes 4587520 | tf_op jit(solution)/shard_map/reshape | solution.py:77
  23.9 12.6 %copy.17 = bf16[2,2,128,2240]{2,1,3,0:T(2,128)(2,1)} copy(bf16[2,2,128,2240]{2,3,1,0:T(8,128)(2,1)} %param.11) | data formatting | bytes 4587520 | tf_op args[2]
  36.5 6.2 %reshape.38 = bf16[2,256,20,112]{1,3,2,0:T(8,128)(2,1)} reshape(bf16[2,2,128,2240]{2,1,3,0:T(2,128)(2,1)} %copy.17) | data formatting | bytes 4587520 | tf_op jit(solution)/shard_map/reshape | solution.py:78
  42.7 3.8 fusion.10
  46.5 5.6 %reshape.39 = f32[2,250880]{1,0:T(2,128)} reshape(f32[2,20,112,112]{3,2,1,0:T(8,128)} %fusion.10) | data formatting | bytes 4014080 | tf_op jit(solution)/shard_map/reshape | solution.py:82
  52.1 0.6 dynamic-slice
  52.7 1.3 maximum_dynamic-update-slice_fusion
  55.9 0.6 fusion.9
  56.6 48.6 %all-reduce.3.cloned.1.call-done = f32[2,250880]{1,0:T(2,128)} async-done(((f32[2,250880]{1,0:T(2,128)}), f32[2,250880]{1,0:T(2,128)}) %all-reduce.3.cloned.1.call-update) | async-done | bytes 2007056 | tf_op jit(solution)/shard_map/psum | solution.py:85
  105.1 8.0 %fusion.8 = (f32[1,250880]{1,0:T(1,128)S(1)}, f32[1,1,250880]{2,1,0:T(1,128)}, f32[1,1,250880]{2,1,0:T(1,128)}, f32[1,250880]{1,0:T(1,128)}) fusion(f32[2,250880]{1,0:T(2,128)} %all-reduce.3.cloned.1.call-done, f32[]{:T(128)} %bitcast.7, f32[]{:T(128)} %bitcast.6, f32[]{:T(128)} %bitcast.5, f32[]{:T(128)} %bitcast.12, f32[]{:T(128)} %bitcast.11), kind=kLoop, calls=%fused_computation.27 | loop fusion | flops 1505280 | bytes 6021140 | tf_op jit(solution)/shard_map/slice | solution.py:47
  113.1 0.7 all-gather.9.cloned.1.call-update
  113.9 0.5 all-gather.7.cloned.1.call-update
  114.4 11.9 %all-reduce = f32[4]{0:T(128)S(1)} all-reduce(f32[4]{0:T(128)S(1)} %get-tuple-element.81), channel_id=2, replica_groups=mesh['grp'=2,'frm'=4,'row'=4] {'frm'}, use_global_device_ids=true, to_apply=%add | all-reduce | flops 4 | bytes 32
  126.4 10.1 %copy.20 = bf16[2,2,128,2240]{2,1,3,0:T(2,128)(2,1)S(1)} copy(bf16[2,2,128,2240]{2,3,1,0:T(8,128)(2,1)S(1)} %broadcast_maximum_fusion) | data formatting | bytes 4587520 | tf_op jit(solution)/shard_map/jit(relu)/max | solution.py:92
  136.5 2.7 reshape.40
  139.3 51.7 %all-gather.11.cloned.1.call-done = f32[4,1,250880]{2,1,0:T(1,128)} async-done(((f32[1,1,250880]{2,1,0:T(1,128)}), f32[4,1,250880]{2,1,0:T(1,128)}) %all-gather.11.cloned.1.call-update) | async-done | bytes 4014096 | tf_op jit(solution)/shard_map/all_gather | solution.py:13
  191.1 5.5 %copy.28 = f32[4,1,250880]{2,0,1:T(4,128)} copy(f32[4,1,250880]{2,1,0:T(1,128)} %all-gather.11.cloned.1.call-done) | data formatting | bytes 8028160
  196.5 72.4 %all-gather.9.cloned.1.call-done = f32[4,1,250880]{2,1,0:T(1,128)} async-done(((f32[1,1,250880]{2,1,0:T(1,128)}), f32[4,1,250880]{2,1,0:T(1,128)}) %all-gather.9.cloned.1.call-update) | async-done | bytes 4014096 | tf_op jit(solution)/shard_map/all_gather | solution.py:13
  268.9 5.5 %copy.29 = f32[4,1,250880]{2,0,1:T(4,128)} copy(f32[4,1,250880]{2,1,0:T(1,128)} %all-gather.9.cloned.1.call-done) | data formatting | bytes 8028160
  277.9 3.6 add_add_fusion.1
  281.5 1.9 stack.9
  283.8 3.0 stack.10
  286.7 2.7 copy.19
  289.4 3.7 fusion
  293.2 0.7 fusion.2
  293.9 2.4 copy.21
  296.7 153.4 %all-gather.7.cloned.1.call-done = bf16[2240,2240]{1,0:T(8,128)(2,1)} async-done(((bf16[560,2240]{1,0:T(8,128)(2,1)}), bf16[2240,2240]{1,0:T(8,128)(2,1)}) %all-gather.7.cloned.1.call-update) | async-done | bytes 10035216 | tf_op jit(solution)/shard_map/all_gather | solution.py:103
  450.1 13.4 %convolution_convert_fusion = bf16[512,2240]{0,1:T(8,128)(2,1)} fusion(bf16[512,2240]{0,1:T(8,128)(2,1)S(1)} %bitcast.74, bf16[2240,2240]{1,0:T(8,128)(2,1)} %all-gather.7.cloned.1.call-done), kind=kOutput, calls=%fused_computation.10 | convolution fusion | flops 5139169280 | bytes 14622720 | tf_op jit(solution)/shard_map/dot_general | solution.py:101
  463.6 4.8 %reshape.42 = bf16[2,2,128,2240]{2,1,0,3:T(2,128)(2,1)S(1)} reshape(bf16[512,2240]{0,1:T(8,128)(2,1)} %convolution_convert_fusion) | data formatting | bytes 4587520 | tf_op jit(solution)/shard_map/reshape | solution.py:106
  468.4 1.7 copy.22
  (29 shorter events, 1.6 us)
Async XLA Ops:
  6.5 98.6 %all-reduce.3.cloned.1.call-start = ((), (), s32[]{:S(2)}) async-start(), calls=%async_computation | async-start | bytes 4014080 | tf_op jit(solution)/shard_map/psum | solution.py:85
  46.5 5.6 %copy-start.3 = (s32[2]{0:T(128)S(1)}, s32[2]{0:T(128)}, u32[]{:S(2)}) copy-start(s32[2]{0:T(128)} %param.13) | copy-start | bytes 28
  46.5 5.7 %copy-start.5 = (u32[32]{0:T(128)S(1)}, u32[32]{0:T(128)}, u32[]{:S(2)}) copy-start(u32[32]{0:T(128)} %constant.52) | copy-start | bytes 388
  46.5 9.4 %copy-start.4 = (s32[2]{0:T(128)S(1)}, s32[2]{0:T(128)}, u32[]{:S(2)}) copy-start(s32[2]{0:T(128)} %param.12) | copy-start | bytes 28
  52.0 139.0 %all-gather.11.cloned.1.call-start = ((), (), s32[]{:S(2)}) async-start(), calls=%async_computation.3 | async-start | bytes 5017600 | tf_op jit(solution)/shard_map/all_gather | solution.py:13
  113.1 13.2 %copy-start.1 = (bf16[2,2,128,2240]{2,3,1,0:T(8,128)(2,1)S(1)}, bf16[2,2,128,2240]{2,3,1,0:T(8,128)(2,1)}, u32[]{:S(2)}) copy-start(bf16[2,2,128,2240]{2,3,1,0:T(8,128)(2,1)} %param.9) | copy-start | bytes 6881284
  113.1 155.8 %all-gather.9.cloned.1.call-start = ((), (), s32[]{:S(2)}) async-start(), calls=%async_computation.2 | async-start | bytes 5017600 | tf_op jit(solution)/shard_map/all_gather | solution.py:13
  113.8 336.3 %all-gather.7.cloned.1.call-start = ((), (), s32[]{:S(2)}) async-start(), calls=%async_computation.1 | async-start | bytes 12902400 | tf_op jit(solution)/shard_map/all_gather | solution.py:103
  136.5 2.8 copy-start.2
  283.8 5.7 %copy-start = (bf16[2,256,20,112]{1,3,2,0:T(8,128)(2,1)S(1)}, bf16[2,256,20,112]{1,3,2,0:T(8,128)(2,1)}, u32[]{:S(2)}) copy-start(bf16[2,256,20,112]{1,3,2,0:T(8,128)(2,1)} %reshape.40) | copy-start | bytes 6881284
Sparse Core Ops, SparseCore 0:
  52.2 52.9 all-reduce.2
  113.2 77.8 all-gather.10
  192.6 76.2 all-gather.8
  270.3 179.7 all-gather.6
where the time goes:
time: 477 us
  waiting for transfers between devices  327 us (69%)
  local copies, waits for them, and re-layouts  82.4 us (17%)
  matrix products  21 us (4%)
  between operations  18.3 us (4%)
  other arithmetic  15.5 us (3%)
  blocking collectives  11.9 us (2%)
    all_gather x1, waiting for transfers between devices, local(): lax.all_gather(out_weight, 'frm', axis=0, tiled=True)  153 us
    all_gather x2, waiting for transfers between devices, entering(): gathered = jax.tree.map(lambda a: lax.all_gather(a, axis), part)  124 us
    psum x1, waiting for transfers between devices, local(): summed = lax.psum(partial_value, 'row')  48.6 us
    unnamed x18, local copies, waits for them, and re-layouts  24.6 us
    dot_general x1, matrix products, local(): jnp.dot(normed, lax.all_gather(out_weight, 'frm', axis=0, tiled=True), pr...  13.4 us
    unnamed x1, blocking collectives  11.9 us
    max x1, local copies, waits for them, and re-layouts, local(): key_pos = jax.nn.relu(keys).reshape(frames, tokens, HEADS, HD)  10.3 us
    max x1, local copies, waits for them, and re-layouts, local(): jax.nn.relu(queries).reshape(frames, tokens, HEADS, HD).astype(jnp.float32)  10.1 us
  transfers between devices with their start and end apart: 4, of which 4 were waited for; matrix products, arithmetic and copies ran while one was open for 10% of the time, Pallas kernels for 0%

commit v1 on v0

--- a/solution.py
+++ b/solution.py
@@ -6,6 +6,23 @@
 HEADS = 20
 HD = 112
 norm_eps = 1e-06
+
+
+def unite_meshes(local_block):
+    ax_name = "frm"
+    b_next = lax.axis_size(ax_name)
+    last = lax.axis_index(ax_name)
+    back, u1 = (b_next, last)
+    far_arr, now = (local_block, 1)
+    while now < back:
+        value_now = lax.ppermute(
+            far_arr, axis_name=ax_name, perm=[(c, c ^ now) for c in range(back)]
+        )
+        b_now = jnp.concatenate([far_arr, value_now], axis=0)
+        small = jnp.concatenate([value_now, far_arr], axis=0)
+        far_arr = jnp.where(u1 & now == 0, b_now, small)
+        now = 2 * now
+    return far_arr
 
 
 def entering(part, axis, combine, identity):
@@ -98,11 +115,7 @@
     normed = (
         (attended * inv_rms * gain_table).astype(jnp.bfloat16).reshape(frames * tokens, model_width)
     )
-    projected = jnp.dot(
-        normed,
-        lax.all_gather(out_weight, "frm", axis=0, tiled=True),
-        preferred_element_type=jnp.float32,
-    )
+    projected = jnp.dot(normed, unite_meshes(out_weight), preferred_element_type=jnp.float32)
     return projected.astype(jnp.bfloat16).reshape(frames, lat_rows, lat_cols, model_width)
 
 

time: 477 us -> 561 us (1.18)
  blocking collectives: 11.9 us -> 126 us
  waiting for transfers between devices: 327 us -> 289 us
  other arithmetic: 15.5 us -> 23.6 us
    all_gather x1 -> x0, waiting for transfers between devices: 153 us -> none  [local(): lax.all_gather(out_weight, 'frm', axis=0, tiled=True)]
    unnamed x1, blocking collectives: 11.9 us -> 126 us
    all_gather x2, waiting for transfers between devices: 124 us -> 184 us  [entering(): gathered = jax.tree.map(lambda a: lax.all_gather(a, axis), part)]
    ppermute x0 -> x2, waiting for transfers between devices: none -> 56.3 us  [unite_meshes(): lax.ppermute(far_arr, axis_name=ax_name, perm=[(c, c ^ now) for c in rang...]
    select_n x0 -> x1, other arithmetic: none -> 7.91 us  [unite_meshes(): far_arr = jnp.where(u1 & now == 0, b_now, small)]
  transfers between devices with their start and end apart: 4 -> 5, of which waited for: 4 -> 3; matrix products, arithmetic and copies ran while one was open for 10% -> 9% of each run, Pallas kernels for 0% -> 0%
where the time goes in v1:
time: 561 us; the launch traced here: 560 us
  waiting for transfers between devices  289 us (52%)
  blocking collectives  126 us (22%)
  local copies, waits for them, and re-layouts  82.3 us (15%)
  other arithmetic  23.6 us (4%)
  matrix products  18.9 us (3%)
  between operations  18.5 us (3%)
    all_gather x2, waiting for transfers between devices, entering(): gathered = jax.tree.map(lambda a: lax.all_gather(a, axis), part)  184 us
    unnamed x1, blocking collectives  126 us
    ppermute x2, waiting for transfers between devices, unite_meshes(): lax.ppermute(far_arr, axis_name=ax_name, perm=[(c, c ^ now) for c in rang...  56.3 us
    psum x1, waiting for transfers between devices, local(): summed = lax.psum(partial_value, 'row')  48.6 us
    unnamed x18, local copies, waits for them, and re-layouts  24.7 us
    dot_general x1, matrix products, local(): jnp.dot(normed, unite_meshes(out_weight), preferred_element_type=jnp.floa...  11.4 us
  transfers between devices with their start and end apart: 5, of which 3 were waited for; matrix products, arithmetic and copies ran while one was open for 9% of the time, Pallas kernels for 0%

profile of v1, /device:TPU:0, one launch (start us, length us, event | category | flops | bytes accessed | tf_op | source)
XLA Modules:
  0.0 560.5 jit_solution(14881086034674286296)
XLA Ops:
  6.5 1.8 broadcast_maximum_fusion.1
  8.3 10.3 %copy.16 = bf16[2,2,128,2240]{2,1,3,0:T(2,128)(2,1)} copy(bf16[2,2,128,2240]{2,3,1,0:T(8,128)(2,1)S(1)} %broadcast_maximum_fusion.1) | data formatting | bytes 4587520 | tf_op jit(solution)/shard_map/jit(relu)/max | solution.py:94
  18.7 5.2 reshape.37
  23.9 12.6 %copy.17 = bf16[2,2,128,2240]{2,1,3,0:T(2,128)(2,1)} copy(bf16[2,2,128,2240]{2,3,1,0:T(8,128)(2,1)} %param.11) | data formatting | bytes 4587520 | tf_op args[2]
  36.5 6.2 %reshape.38 = bf16[2,256,20,112]{1,3,2,0:T(8,128)(2,1)} reshape(bf16[2,2,128,2240]{2,1,3,0:T(2,128)(2,1)} %copy.17) | data formatting | bytes 4587520 | tf_op jit(solution)/shard_map/reshape | solution.py:95
  42.7 3.8 fusion.19
  46.5 5.5 reshape.39
  52.1 0.6 dynamic-slice
  52.7 1.2 maximum_dynamic-update-slice_fusion
  55.9 0.6 fusion.18
  56.5 48.6 %all-reduce.3.cloned.1.call-done = f32[2,250880]{1,0:T(2,128)} async-done(((f32[2,250880]{1,0:T(2,128)}), f32[2,250880]{1,0:T(2,128)}) %all-reduce.3.cloned.1.call-update) | async-done | bytes 2007056 | tf_op jit(solution)/shard_map/psum | solution.py:102
  105.1 8.2 %fusion.17 = (f32[1,250880]{1,0:T(1,128)S(1)}, f32[1,1,250880]{2,1,0:T(1,128)}, f32[1,1,250880]{2,1,0:T(1,128)}, f32[1,250880]{1,0:T(1,128)}) fusion(f32[2,250880]{1,0:T(2,128)} %all-reduce.3.cloned.1.call-done, f32[]{:T(128)} %bitcast.7, f32[]{:T(128)} %bitcast.6, f32[]{:T(128)} %bitcast.5, f32[]{:T(128)} %bitcast.12, f32[]{:T(128)} %bitcast.11), kind=kLoop, calls=%fused_computation.37 | loop fusion | flops 1505280 | bytes 6021140 | tf_op jit(solution)/shard_map/slice | solution.py:64
  113.3 0.7 all-gather.6.cloned.1.call-update
  114.0 1.6 collective-permute-start
  115.6 126.1 %all-reduce = f32[4]{0:T(128)S(1)} all-reduce(f32[4]{0:T(128)S(1)} %get-tuple-element.81), channel_id=2, replica_groups=mesh['grp'=2,'frm'=4,'row'=4] {'frm'}, use_global_device_ids=true, to_apply=%add | all-reduce | flops 4 | bytes 32
  241.8 10.1 %copy.20 = bf16[2,2,128,2240]{2,1,3,0:T(2,128)(2,1)S(1)} copy(bf16[2,2,128,2240]{2,3,1,0:T(8,128)(2,1)S(1)} %broadcast_maximum_fusion) | data formatting | bytes 4587520 | tf_op jit(solution)/shard_map/jit(relu)/max | solution.py:109
  251.9 2.7 reshape.40
  254.7 7.9 %maximum_select_fusion.2 = bf16[1120,2240]{1,0:T(8,128)(2,1)} fusion(bf16[560,2240]{1,0:T(8,128)(2,1)} %collective-permute-done, bf16[560,2240]{1,0:T(8,128)(2,1)} %param.14, pred[]{:T(512)S(6)} %eq.7), kind=kLoop, calls=%fused_computation.13 | loop fusion | flops 22579200 | bytes 10035201 | tf_op jit(solution)/shard_map/jit(_where)/select_n | solution.py:23
  262.7 5.5 copy.28
  268.2 183.6 %all-gather.6.cloned.1.call-done = f32[4,1,250880]{2,1,0:T(1,128)} async-done(((f32[1,1,250880]{2,1,0:T(1,128)}), f32[4,1,250880]{2,1,0:T(1,128)}) %all-gather.6.cloned.1.call-update) | async-done | bytes 4014096 | tf_op jit(solution)/shard_map/all_gather | solution.py:30
  451.8 5.5 copy.29
  460.9 3.6 add_add_fusion.1
  464.5 1.8 stack.9
  466.7 3.0 stack.10
  469.7 2.6 copy.19
  472.3 3.7 fusion.7
  476.1 0.7 fusion.9
  476.8 2.4 copy.21
  479.7 56.3 %collective-permute-done.1 = bf16[1120,2240]{1,0:T(8,128)(2,1)} collective-permute-done((bf16[1120,2240]{1,0:T(8,128)(2,1)}, bf16[1120,2240]{1,0:T(8,128)(2,1)}, u32[]{:S(2)}, u32[]{:S(2)}) %collective-permute-start.1) | collective-permute-done | bytes 5017632 | tf_op jit(solution)/shard_map/ppermute | solution.py:18
  536.0 11.4 %fusion.10 = bf16[512,2240]{0,1:T(8,128)(2,1)} fusion(bf16[512,2240]{0,1:T(8,128)(2,1)S(1)} %bitcast.73, bf16[1120,2240]{1,0:T(8,128)(2,1)} %collective-permute-done.1, bf16[1120,2240]{1,0:T(8,128)(2,1)} %maximum_select_fusion.2, pred[]{:T(512)S(6)} %eq.6), kind=kOutput, calls=%fused_computation.19 | convolution fusion | flops 5184327680 | bytes 14622721 | tf_op jit(solution)/shard_map/dot_general | solution.py:118
  547.4 4.8 reshape.42
  552.2 1.7 copy.22
  (31 shorter events, 1.6 us)
Async XLA Ops:
  6.5 98.6 %all-reduce.3.cloned.1.call-start = ((), (), s32[]{:S(2)}) async-start(), calls=%async_computation | async-start | bytes 4014080 | tf_op jit(solution)/shard_map/psum | solution.py:102
  46.5 5.6 %copy-start.3 = (s32[2]{0:T(128)S(1)}, s32[2]{0:T(128)}, u32[]{:S(2)}) copy-start(s32[2]{0:T(128)} %param.13) | copy-start | bytes 28
  46.5 5.7 %copy-start.5 = (u32[32]{0:T(128)S(1)}, u32[32]{0:T(128)}, u32[]{:S(2)}) copy-start(u32[32]{0:T(128)} %constant.56) | copy-start | bytes 388
  46.5 9.4 %copy-start.4 = (s32[2]{0:T(128)S(1)}, s32[2]{0:T(128)}, u32[]{:S(2)}) copy-start(s32[2]{0:T(128)} %param.12) | copy-start | bytes 28
  52.0 210.6 %all-gather.8.cloned.1.call-start = ((), (), s32[]{:S(2)}) async-start(), calls=%async_computation.2 | async-start | bytes 5017600 | tf_op jit(solution)/shard_map/all_gather | solution.py:30
  105.1 136.6 %copy-start.1 = (bf16[2,2,128,2240]{2,3,1,0:T(8,128)(2,1)S(1)}, bf16[2,2,128,2240]{2,3,1,0:T(8,128)(2,1)}, u32[]{:S(2)}) copy-start(bf16[2,2,128,2240]{2,3,1,0:T(8,128)(2,1)} %param.9) | copy-start | bytes 6881284
  113.3 338.5 %all-gather.6.cloned.1.call-start = ((), (), s32[]{:S(2)}) async-start(), calls=%async_computation.1 | async-start | bytes 5017600 | tf_op jit(solution)/shard_map/all_gather | solution.py:30
  114.0 140.7 %collective-permute-start = (bf16[560,2240]{1,0:T(8,128)(2,1)}, bf16[560,2240]{1,0:T(8,128)(2,1)}, u32[]{:S(2)}, u32[]{:S(2)}) collective-permute-start(bf16[560,2240]{1,0:T(8,128)(2,1)} %param.14), channel_id=1, source_target_pairs={{0,4},{4,0},{8,12},{12,8},{1,5},{5,1},{9,13},{13,9},{2,6},{6,2},{1... | collective-permute-start | bytes 7526408 | tf_op jit(solution)/shard_map/ppermute | solution.py:18
  251.9 2.8 copy-start.2
  262.6 273.3 %collective-permute-start.1 = (bf16[1120,2240]{1,0:T(8,128)(2,1)}, bf16[1120,2240]{1,0:T(8,128)(2,1)}, u32[]{:S(2)}, u32[]{:S(2)}) collective-permute-start(bf16[1120,2240]{1,0:T(8,128)(2,1)} %maximum_select_fusion.2), channel_id=1, source_target_pairs={{0,8},{4,12},{8,0},{12,4},{1,9},{5,13},{9,1},{13,5},{2,10},{6,14},... | collective-permute-start | bytes 15052808 | tf_op jit(solution)/shard_map/ppermute | solution.py:18
  466.7 5.6 %copy-start = (bf16[2,256,20,112]{1,3,2,0:T(8,128)(2,1)S(1)}, bf16[2,256,20,112]{1,3,2,0:T(8,128)(2,1)}, u32[]{:S(2)}) copy-start(bf16[2,256,20,112]{1,3,2,0:T(8,128)(2,1)} %reshape.40) | copy-start | bytes 6881284
Sparse Core Ops, SparseCore 0:
  52.1 52.9 all-reduce.2
  113.4 122.2 all-gather.7
  237.3 214.4 all-gather.5
